TPU v7x, 256 devices: a whole 4x4x8 slice. The times are simulated.
256 devices in a mesh: rep: 32 (over z, y), tp: 8 (over x, core).
Axes of the slice: x: 4, y: 4, z: 8, core: 2. Of those that a mesh axis runs over, the one named last changes fastest.
Arguments:
- image_grads: bfloat16 [512, 48, 1280], P('rep', 'tp'), may hold values from -6 to 6
- dest_rank: int32 [512], P('rep'), may hold values from 0 to 31, as said below
- dest_slot: int32 [512], P('rep'), may hold values from 0 to 31, as said below
- saved_inputs: bfloat16 [1024, 48, 1280], P('rep'), may hold values from -6 to 6
- up_weight: bfloat16 [1280, 5120], P(None, 'tp'), may hold values from -0.15625 to 0.15625
- down_weight: bfloat16 [5120, 1280], P('tp'), may hold values from -0.078125 to 0.078125
- norm_gain: float32 [1280], replicated, may hold values from 0.25 to 1.75
Outputs:
- input_grads: bfloat16 [1024, 48, 1280], P('rep', 'tp')
- up_grads: float32 [1280, 5120], P('rep', 'tp')
- down_grads: float32 [5120, 1280], P('tp', 'rep')
- gain_grads: float32 [1280], replicated
Inputs may be any that keep to these rules, and one draw needn't show every extreme that they name: `dest_rank`: the images of one index of rep go to different owners; each owner receives at most 32 images, and some owner receives exactly 32 in every draw. `dest_slot`: the images that one owner receives have distinct slots 0, 1, ... up to their count less one; other slots hold no image.
All inputs are finite; a program needn't handle non-finite values.
Results may differ from a plain program's by a relative error of at most 0.015.
Values may be sent and summed in bfloat16 or wider, within the bound.
A program may use at most 128 MiB of HBM per device.

v0:
```python
import jax
import jax.numpy as jnp
from jax import lax
from jax.sharding import Mesh
from jax.sharding import PartitionSpec as P

REP = ("rep_0", "rep_1")
epsilon = 1e-05
gelu_c = 0.7978845608028654
gelu_a = 0.044715


def scatter_axes(value, axes, dim):
    if not axes:
        return value
    nearer = lax.psum_scatter(value, axes[0], scatter_dimension=dim, tiled=True)
    return scatter_axes(nearer, axes[1:], dim)


def sent_to_all(value, axis):
    copies = jnp.broadcast_to(value, (lax.axis_size(axis), *value.shape))
    return lax.all_to_all(copies, axis, split_axis=0, concat_axis=0, tiled=True)


def of_everyone(value, axis):
    everything = sent_to_all(value, axis)
    return jnp.sum(everything, axis=0)


def gelu_value(preact):
    inner = jnp.tanh(gelu_c * (preact + gelu_a * preact**3))
    return 0.5 * preact * (1.0 + inner)


def gelu_slope(preact):
    inner = jnp.tanh(gelu_c * (preact + gelu_a * preact**3))
    return 0.5 * (1.0 + inner) + 0.5 * preact * (1.0 - inner * inner) * gelu_c * (
        1.0 + 3.0 * gelu_a * preact * preact
    )


def outbound(images, dest_rank, dest_slot, groups, capacity):
    rank_ids = jnp.arange(groups, dtype=jnp.int32)
    one_hot = dest_rank[None, :] == rank_ids[:, None]
    packed = jnp.einsum(
        "ek,kpd->epd", one_hot.astype(jnp.bfloat16), images, preferred_element_type=jnp.float32
    ).astype(jnp.bfloat16)
    present = jnp.any(one_hot, axis=1)
    slot_sent = jnp.sum(jnp.where(one_hot, dest_slot[None, :], 0), axis=1) + jnp.where(
        present, 0, capacity
    )
    return (packed, slot_sent)


def compact(inbound, slot_recv, capacity):
    slot_ids = jnp.arange(capacity, dtype=jnp.int32)
    picker = (slot_recv[None, :] == slot_ids[:, None]).astype(jnp.bfloat16)
    return jnp.einsum("ce,epd->cpd", picker, inbound, preferred_element_type=jnp.float32).astype(
        jnp.bfloat16
    )


def local(image_grads, dest_rank, dest_slot, saved_inputs, up_weight, down_weight, norm_gain):
    groups = lax.axis_size(REP)
    capacity = saved_inputs.shape[0]
    patches = saved_inputs.shape[1]
    width = saved_inputs.shape[2]
    slab = image_grads.shape[1]
    packed, slot_sent = outbound(image_grads, dest_rank, dest_slot, groups, capacity)
    inbound, slot_recv = (
        lax.all_to_all(packed, REP, split_axis=0, concat_axis=0, tiled=True),
        lax.all_to_all(slot_sent, REP, split_axis=0, concat_axis=0, tiled=True),
    )
    routed = lax.all_gather(compact(inbound, slot_recv, capacity), "tp", axis=1, tiled=True)
    rows = capacity * patches
    grads = routed.reshape(rows, width)
    values = saved_inputs.reshape(rows, width).astype(jnp.float32)
    mean_v = jnp.mean(values, axis=1, keepdims=True)
    var_v = jnp.mean((values - mean_v) ** 2, axis=1, keepdims=True)
    inv_std = 1.0 / jnp.sqrt(var_v + epsilon)
    centred = (values - mean_v) * inv_std
    normed = (centred * norm_gain[None, :]).astype(jnp.bfloat16)
    preact = jnp.dot(normed, up_weight, preferred_element_type=jnp.float32)
    hidden = gelu_value(preact).astype(jnp.bfloat16)
    grad_hidden = jnp.dot(grads, down_weight.T, preferred_element_type=jnp.float32)
    grad_pre = (grad_hidden * gelu_slope(preact)).astype(jnp.bfloat16)
    down_local = jnp.dot(hidden.T, grads, preferred_element_type=jnp.float32)
    up_local = jnp.dot(normed.T, grad_pre, preferred_element_type=jnp.float32)
    partial_normed = jnp.dot(grad_pre, up_weight.T, preferred_element_type=jnp.float32)
    up_grads, down_grads = (
        scatter_axes(up_local.astype(jnp.bfloat16), REP, 0).astype(jnp.float32),
        scatter_axes(down_local.astype(jnp.bfloat16), REP, 1).astype(jnp.float32),
    )
    start = lax.axis_index("tp") * slab
    grad_normed = lax.psum(partial_normed.astype(jnp.bfloat16), "tp").astype(jnp.float32)
    gain_grads = of_everyone(jnp.sum(grad_normed * centred, axis=0), REP)
    scaled = grad_normed * norm_gain[None, :]
    first = jnp.mean(scaled, axis=1, keepdims=True)
    second = jnp.mean(scaled * centred, axis=1, keepdims=True)
    result = grads.astype(jnp.float32) + inv_std * (scaled - first - centred * second)
    result = result.reshape(capacity, patches, width)
    input_grads = lax.dynamic_slice_in_dim(result, start, slab, 1).astype(jnp.bfloat16)
    return (input_grads, up_grads, down_grads, gain_grads)


def solution(mesh):
    split = Mesh(mesh.devices.reshape(8, 4, mesh.shape["tp"]), ("rep_0", "rep_1", "tp"))
    return jax.shard_map(
        local,
        mesh=split,
        in_specs=(
            P(REP, "tp", None),
            P(REP),
            P(REP),
            P(REP, None, None),
            P(None, "tp"),
            P("tp", None),
            P(),
        ),
        out_specs=(P(REP, "tp", None), P(REP, "tp"), P("tp", REP), P()),
        check_vma=False,
    )
```

profile of v0, /device:TPU:2, one launch (start us, length us, event | category | flops | bytes accessed | tf_op | source)
XLA Modules:
  0.0 318.9 jit_solution(2042661000471552826)
XLA Ops:
  7.2 0.9 fusion.27
  9.5 11.5 %all-to-all-start = ((s32[32,1,1]{2,1,0:T(1,128)}), s32[32,1,1]{2,1,0:T(1,128)S(1)}, u32[]{:S(2)}, u32[]{:S(2)}) async-start(s32[32,1,1]{2,1,0:T(1,128)} %copy.29), calls=%async_computation | async-start | bytes 32768 | tf_op jit(solution)/shard_map/all_to_all | solution.py:72
  21.0 1.4 convolution_convert_fusion.4
  22.4 1.1 copy.30
  23.5 7.2 %all-to-all-done = s32[32,1,1]{2,1,0:T(1,128)S(1)} async-done(((s32[32,1,1]{2,1,0:T(1,128)}), s32[32,1,1]{2,1,0:T(1,128)S(1)}, u32[]{:S(2)}, u32[]{:S(2)}) %all-to-all-start) | async-done | bytes 160 | tf_op jit(solution)/shard_map/all_to_all | solution.py:72
  30.7 3.9 %all-to-all-start.1 = ((bf16[32,6,1280]{2,1,0:T(8,128)(2,1)}), bf16[32,6,1280]{2,1,0:T(8,128)(2,1)S(1)}, u32[]{:S(2)}, u32[]{:S(2)}) async-start(bf16[32,6,1280]{2,1,0:T(8,128)(2,1)} %copy.30), calls=%async_computation.1 | async-start | bytes 1310720 | tf_op jit(solution)/shard_map/all_to_all | solution.py:71
  35.3 18.5 %all-to-all-done.1 = bf16[32,6,1280]{2,1,0:T(8,128)(2,1)S(1)} async-done(((bf16[32,6,1280]{2,1,0:T(8,128)(2,1)}), bf16[32,6,1280]{2,1,0:T(8,128)(2,1)S(1)}, u32[]{:S(2)}, u32[]{:S(2)}) %all-to-all-start.1) | async-done | bytes 491552 | tf_op jit(solution)/shard_map/all_to_all | solution.py:71
  53.8 1.1 convolution_convert_fusion.3
  55.1 2.7 convert_reduce_fusion
  57.9 3.3 %multiply_reduce_fusion = f32[32,48]{1,0:T(8,128)S(1)} fusion(bf16[32,48,1280]{2,1,0:T(8,128)(2,1)} %param.10, f32[32,48]{1,0:T(8,128)S(1)} %broadcast_multiply_fusion), kind=kLoop, calls=%fused_computation.13 | loop fusion | flops 7862784 | bytes 3944448 | tf_op jit(solution)/shard_map/reduce_sum | solution.py:79
  61.3 3.0 multiply_convert_fusion
  64.3 2.0 copy-done.2
  66.3 5.2 %fusion.34 = f32[1536,640]{1,0:T(8,128)} fusion(bf16[1536,1280]{1,0:T(8,128)(2,1)S(1)} %multiply_convert_fusion, bf16[1280,640]{1,0:T(8,128)(2,1)S(1)} %copy-done), kind=kOutput, calls=%fused_computation.56 | convolution fusion | flops 2516582400 | bytes 9502720 | tf_op jit(solution)/shard_map/dot_general | solution.py:83
  71.5 12.3 %all-gather.2.cloned.1.call-done = bf16[32,48,1280]{2,0,1:T(8,128)(2,1)} async-done(((bf16[32,6,1280]{2,0,1:T(8,128)(2,1)}), bf16[32,48,1280]{2,0,1:T(8,128)(2,1)}) %all-gather.2.cloned.1.call-update) | async-done | bytes 3932176 | tf_op jit(solution)/shard_map/all_gather | solution.py:74
  83.8 4.4 %copy.32 = bf16[32,48,1280]{2,1,0:T(8,128)(2,1)S(1)} copy(bf16[32,48,1280]{2,0,1:T(8,128)(2,1)} %all-gather.2.cloned.1.call-done) | data formatting | bytes 7864320 | tf_op jit(solution)/shard_map/all_gather | solution.py:74
  88.2 1.9 copy-done.1
  90.1 5.1 %convolution_convert_fusion.1 = bf16[640,1280]{0,1:T(8,128)(2,1)} fusion(bf16[1536,1280]{1,0:T(8,128)(2,1)S(1)} %bitcast.34, f32[1536,640]{1,0:T(8,128)S(1)} %copy-done.5), kind=kOutput, calls=%fused_computation.28 | convolution fusion | flops 2526248960 | bytes 9502720 | tf_op jit(solution)/shard_map/dot_general | solution.py:87
  95.5 8.2 %fusion.17 = bf16[1536,640]{1,0:T(8,128)(2,1)S(1)} fusion(f32[1536,640]{1,0:T(8,128)} %fusion.34, bf16[1536,1280]{1,0:T(8,128)(2,1)} %bitcast.35, bf16[640,1280]{1,0:T(8,128)(2,1)S(1)} %copy-done.4), kind=kOutput, calls=%fused_computation.26 | convolution fusion | flops 2535260160 | bytes 11468800 | tf_op jit(solution)/shard_map/dot_general | solution.py:85
  103.7 1.3 copy-done.6
  104.9 4.7 %convolution_convert_fusion = bf16[1536,1280]{1,0:T(8,128)(2,1)} fusion(bf16[1536,640]{1,0:T(8,128)(2,1)S(1)} %fusion.17, bf16[1280,640]{1,0:T(8,128)(2,1)S(1)} %copy-done), kind=kOutput, calls=%fused_computation.14 | convolution fusion | flops 2518548480 | bytes 7536640 | tf_op jit(solution)/shard_map/dot_general | solution.py:89
  109.7 7.2 %convolution_convert_fusion.2 = bf16[1280,640]{1,0:T(8,128)(2,1)} fusion(bf16[1536,1280]{1,0:T(8,128)(2,1)} %copy-done.2, bf16[1536,640]{1,0:T(8,128)(2,1)} %copy-done.6), kind=kOutput, calls=%fused_computation.29 | convolution fusion | flops 2517401600 | bytes 7536640 | tf_op jit(solution)/shard_map/dot_general | solution.py:88
  117.0 20.4 %reduce-scatter.11.cloned.1.call-done = bf16[640,160]{0,1:T(8,128)(2,1)} async-done(((bf16[640,1280]{0,1:T(8,128)(2,1)}), bf16[640,160]{0,1:T(8,128)(2,1)}) %reduce-scatter.11.cloned.1.call-update) | async-done | bytes 204816 | tf_op jit(solution)/shard_map/reduce_scatter | solution.py:16
  137.4 74.8 %all-reduce.4.cloned.1.call-done = bf16[1536,1280]{1,0:T(8,128)(2,1)} async-done(((bf16[1536,1280]{1,0:T(8,128)(2,1)}), bf16[1536,1280]{1,0:T(8,128)(2,1)}) %all-reduce.4.cloned.1.call-update) | async-done | bytes 3932176 | tf_op jit(solution)/shard_map/psum | solution.py:95
  212.2 5.8 %fusion.7 = (f32[1280]{0:T(1024)S(1)}, f32[1536]{0:T(1024)S(1)}, f32[1536]{0:T(1024)S(1)}) fusion(bf16[1536,1280]{1,0:T(8,128)(2,1)} %all-reduce.4.cloned.1.call-done, bf16[32,48,1280]{2,1,0:T(8,128)(2,1)} %param.10, f32[1536]{0:T(1024)S(1)} %div.18, f32[1536]{0:T(1024)S(1)} %sqrt.6, f32[1280]{0:T(1024)S(1)} %copy-done.3), kind=kLoop, calls=%fused_computation.9 | loop fusion | flops 19656448 | bytes 7899136 | tf_op jit(solution)/shard_map/reduce_sum | solution.py:96
  218.8 9.9 %all-to-all-start.2 = ((f32[32,1,1280]{2,1,0:T(1,128)}), f32[32,1,1280]{2,1,0:T(1,128)S(1)}, u32[]{:S(2)}, u32[]{:S(2)}) async-start(f32[32,1,1280]{2,1,0:T(1,128)} %broadcast_in_dim.38), calls=%async_computation.4 | async-start | bytes 327680 | tf_op jit(solution)/shard_map/all_to_all | solution.py:22
  228.7 31.9 %reduce-scatter.9.cloned.1.call-done = bf16[160,640]{1,0:T(8,128)(2,1)} async-done(((bf16[1280,640]{1,0:T(8,128)(2,1)}), bf16[160,640]{1,0:T(8,128)(2,1)}) %reduce-scatter.9.cloned.1.call-update) | async-done | bytes 204816 | tf_op jit(solution)/shard_map/reduce_scatter | solution.py:16
  260.6 6.1 %fusion.5 = bf16[1536,1280]{1,0:T(8,128)(2,1)S(1)} fusion(bf16[1536,1280]{1,0:T(8,128)(2,1)} %all-reduce.4.cloned.1.call-done, bf16[32,48,1280]{2,1,0:T(8,128)(2,1)} %param.10, f32[1536]{0:T(1024)S(1)} %get-tuple-element.7, f32[1536]{0:T(1024)S(1)} %get-tuple-element.8, f32[1280]{0:T(1024)S(1)} %copy-done.3, f32[1536]{0:T(1024)S(1)} %div.18, ...), kind=kLoop, calls=%fused_computation.7 | loop fusion | flops 23592960 | bytes 15758336 | tf_op jit(solution)/shard_map/add | solution.py:100
  266.9 0.9 copy.40
  268.5 16.8 %reduce-scatter.15.cloned.1.call-done = bf16[640,40]{0,1:T(8,128)(2,1)} async-done(((bf16[640,160]{0,1:T(8,128)(2,1)}), bf16[640,40]{0,1:T(8,128)(2,1)}) %reduce-scatter.15.cloned.1.call-update) | async-done | bytes 51216
  285.3 1.5 convert_element_type.66
  286.8 23.8 %reduce-scatter.13.cloned.1.call-done = bf16[40,640]{1,0:T(8,128)(2,1)} async-done(((bf16[160,640]{1,0:T(8,128)(2,1)}), bf16[40,640]{1,0:T(8,128)(2,1)}) %reduce-scatter.13.cloned.1.call-update) | async-done | bytes 51216
  310.6 1.5 convert_element_type.63
  (36 shorter events, 4.7 us)
Async XLA Ops:
  7.2 59.1 %copy-start = (bf16[1280,640]{1,0:T(8,128)(2,1)S(1)}, bf16[1280,640]{1,0:T(8,128)(2,1)}, u32[]{:S(2)}) copy-start(bf16[1280,640]{1,0:T(8,128)(2,1)} %param.11) | copy-start | bytes 4915204
  9.5 21.2 %all-to-all-start = ((s32[32,1,1]{2,1,0:T(1,128)}), s32[32,1,1]{2,1,0:T(1,128)S(1)}, u32[]{:S(2)}, u32[]{:S(2)}) async-start(s32[32,1,1]{2,1,0:T(1,128)} %copy.29), calls=%async_computation | async-start | bytes 32768 | tf_op jit(solution)/shard_map/all_to_all | solution.py:72
  30.7 23.1 %all-to-all-start.1 = ((bf16[32,6,1280]{2,1,0:T(8,128)(2,1)}), bf16[32,6,1280]{2,1,0:T(8,128)(2,1)S(1)}, u32[]{:S(2)}, u32[]{:S(2)}) async-start(bf16[32,6,1280]{2,1,0:T(8,128)(2,1)} %copy.30), calls=%async_computation.1 | async-start | bytes 1310720 | tf_op jit(solution)/shard_map/all_to_all | solution.py:71
  34.6 49.2 %all-gather.2.cloned.1.call-start = ((), (), s32[]{:S(2)}) async-start(), calls=%async_computation.7 | async-start | bytes 4423680 | tf_op jit(solution)/shard_map/all_gather | solution.py:74
  54.8 6.4 %copy-start.3 = (f32[1280]{0:T(1024)S(1)}, f32[1280]{0:T(1024)}, u32[]{:S(2)}) copy-start(f32[1280]{0:T(1024)} %param.13) | copy-start | bytes 15364
  54.9 82.5 %reduce-scatter.11.cloned.1.call-start = ((), (), s32[]{:S(2)}) async-start(), calls=%async_computation.10 | async-start | bytes 1843200 | tf_op jit(solution)/shard_map/reduce_scatter | solution.py:16
  64.3 2.0 copy-start.2
  83.8 6.3 %copy-start.5 = (f32[1536,640]{1,0:T(8,128)S(1)}, f32[1536,640]{1,0:T(8,128)}, u32[]{:S(2)}) copy-start(f32[1536,640]{1,0:T(8,128)} %fusion.34) | copy-start | bytes 11796484
  88.2 1.9 copy-start.1
  90.1 5.4 %copy-start.4 = (bf16[640,1280]{1,0:T(8,128)(2,1)S(1)}, bf16[640,1280]{1,0:T(8,128)(2,1)}, u32[]{:S(2)}) copy-start(bf16[640,1280]{1,0:T(8,128)(2,1)} %param.12) | copy-start | bytes 4915204
  95.2 117.0 %all-reduce.4.cloned.1.call-start = ((), (), s32[]{:S(2)}) async-start(), calls=%async_computation.8 | async-start | bytes 7864320 | tf_op jit(solution)/shard_map/psum | solution.py:95
  103.7 1.3 copy-start.6
  109.7 150.9 %reduce-scatter.9.cloned.1.call-start = ((), (), s32[]{:S(2)}) async-start(), calls=%async_computation.9 | async-start | bytes 1843200 | tf_op jit(solution)/shard_map/reduce_scatter | solution.py:16
  116.9 168.4 %reduce-scatter.15.cloned.1.call-start = ((), (), s32[]{:S(2)}) async-start(), calls=%async_computation.12 | async-start | bytes 256000
  218.8 49.0 %all-to-all-start.2 = ((f32[32,1,1280]{2,1,0:T(1,128)}), f32[32,1,1280]{2,1,0:T(1,128)S(1)}, u32[]{:S(2)}, u32[]{:S(2)}) async-start(f32[32,1,1280]{2,1,0:T(1,128)} %broadcast_in_dim.38), calls=%async_computation.4 | async-start | bytes 327680 | tf_op jit(solution)/shard_map/all_to_all | solution.py:22
  228.6 82.0 %reduce-scatter.13.cloned.1.call-start = ((), (), s32[]{:S(2)}) async-start(), calls=%async_computation.11 | async-start | bytes 256000
Sparse Core Ops, SparseCore 0:
  55.0 28.8 all-gather.1
  95.3 41.9 reduce-scatter.10
  139.7 72.4 all-reduce.3
  214.6 45.9 reduce-scatter.8
  263.0 22.2 reduce-scatter.14
  287.7 22.8 reduce-scatter.12
where the time goes:
time: 319 us
  waiting for transfers between devices  206 us (65%)
  matrix products  32.8 us (10%)
  other arithmetic  26.8 us (8%)
  starting transfers between devices  25.9 us (8%)
  between operations  14.3 us (4%)
  local copies, waits for them, and re-layouts  13.3 us (4%)
    psum x1, waiting for transfers between devices, local(): lax.psum(partial_normed.astype(jnp.bfloat16), 'tp').astype(jnp.float32)  74.8 us
    reduce_scatter x2, waiting for transfers between devices, scatter_axes(): nearer = lax.psum_scatter(value, axes[0], scatter_dimension=dim, tiled=True)  52.3 us
    unnamed x8, waiting for transfers between devices  40.7 us
    all_to_all x1, waiting for transfers between devices, local(): lax.all_to_all(packed, REP, split_axis=0, concat_axis=0, tiled=True)  18.5 us
    all_gather x1, waiting for transfers between devices, local(): lax.all_gather(compact(inbound, slot_recv, capacity), 'tp', axis=1, tiled...  12.3 us
    all_to_all x1, starting transfers between devices, local(): lax.all_to_all(slot_sent, REP, split_axis=0, concat_axis=0, tiled=True)  11.5 us
    all_to_all x1, starting transfers between devices, sent_to_all(): return lax.all_to_all(copies, axis, split_axis=0, concat_axis=0, tiled=True)  9.85 us
    dot_general x1, matrix products, local(): jnp.dot(grads, down_weight.T, preferred_element_type=jnp.float32)  8.16 us
  transfers between devices with their start and end apart: 9, of which 8 were waited for; matrix products, arithmetic and copies ran while one was open for 17% of the time, Pallas kernels for 0%

commit v1 on v0

--- a/solution.py
+++ b/solution.py
@@ -71,7 +71,14 @@
         lax.all_to_all(packed, REP, split_axis=0, concat_axis=0, tiled=True),
         lax.all_to_all(slot_sent, REP, split_axis=0, concat_axis=0, tiled=True),
     )
-    routed = lax.all_gather(compact(inbound, slot_recv, capacity), "tp", axis=1, tiled=True)
+
+    def clear_scenes(v0):
+        a_next = lax.axis_size("tp")
+        before = jnp.concatenate([v0] * a_next, axis=1)
+        met_up = lax.all_to_all(before, "tp", 1, 1, tiled=True)
+        return met_up
+
+    routed = clear_scenes(compact(inbound, slot_recv, capacity))
     rows = capacity * patches
     grads = routed.reshape(rows, width)
     values = saved_inputs.reshape(rows, width).astype(jnp.float32)

time: 319 us -> 261 us (0.82)
  waiting for transfers between devices: 206 us -> 136 us
  local copies, waits for them, and re-layouts: 13.3 us -> 19.1 us
  starting transfers between devices: 25.9 us -> 30.3 us
    reduce_scatter x2, waiting for transfers between devices: 52.3 us -> 14.5 us  [scatter_axes(): nearer = lax.psum_scatter(value, axes[0], scatter_dimension=dim, tiled=True)]
    all_to_all x0 -> x1, waiting for transfers between devices: none -> 29.2 us  [clear_scenes(): met_up = lax.all_to_all(before, 'tp', 1, 1, tiled=True)]
    psum x1, waiting for transfers between devices: 74.8 us -> 48.3 us  [local(): lax.psum(partial_normed.astype(jnp.bfloat16), 'tp').astype(jnp.float32)]
    unnamed x8 -> x7, waiting for transfers between devices: 40.7 us -> 15.6 us
    all_gather x1 -> x0, waiting for transfers between devices: 12.3 us -> none  [local(): lax.all_gather(compact(inbound, slot_recv, capacity), 'tp', axis=1, tiled...]
    unnamed x15 -> x21, local copies, waits for them, and re-layouts: 5.99 us -> 11 us
    all_to_all x0 -> x1, starting transfers between devices: none -> 4.93 us  [clear_scenes(): met_up = lax.all_to_all(before, 'tp', 1, 1, tiled=True)]
    all_to_all x0 -> x1, local copies, waits for them, and re-layouts: none -> 4.42 us  [clear_scenes(): met_up = lax.all_to_all(before, 'tp', 1, 1, tiled=True)]
  transfers between devices with their start and end apart: 9 -> 9, of which waited for: 8 -> 7; matrix products, arithmetic and copies ran while one was open for 17% -> 20% of each run, Pallas kernels for 0% -> 0%
where the time goes in v1:
time: 261 us
  waiting for transfers between devices  136 us (52%)
  matrix products  32.8 us (13%)
  starting transfers between devices  30.3 us (12%)
  other arithmetic  26.8 us (10%)
  local copies, waits for them, and re-layouts  19.1 us (7%)
  between operations  15.4 us (6%)
    psum x1, waiting for transfers between devices, local(): lax.psum(partial_normed.astype(jnp.bfloat16), 'tp').astype(jnp.float32)  48.3 us
    all_to_all x1, waiting for transfers between devices, clear_scenes(): met_up = lax.all_to_all(before, 'tp', 1, 1, tiled=True)  29.2 us
    all_to_all x1, waiting for transfers between devices, local(): lax.all_to_all(packed, REP, split_axis=0, concat_axis=0, tiled=True)  18.5 us
    unnamed x7, waiting for transfers between devices  15.6 us
    reduce_scatter x2, waiting for transfers between devices, scatter_axes(): nearer = lax.psum_scatter(value, axes[0], scatter_dimension=dim, tiled=True)  14.5 us
    all_to_all x1, starting transfers between devices, local(): lax.all_to_all(slot_sent, REP, split_axis=0, concat_axis=0, tiled=True)  11.5 us
    unnamed x21, local copies, waits for them, and re-layouts  11 us
    all_to_all x1, starting transfers between devices, sent_to_all(): return lax.all_to_all(copies, axis, split_axis=0, concat_axis=0, tiled=True)  9.58 us
  transfers between devices with their start and end apart: 9, of which 7 were waited for; matrix products, arithmetic and copies ran while one was open for 20% of the time, Pallas kernels for 0%

profile of v1, /device:TPU:2, one launch (start us, length us, event | category | flops | bytes accessed | tf_op | source)
XLA Modules:
  0.0 260.8 jit_solution(8158484133178665468)
XLA Ops:
  8.0 0.9 fusion.27
  10.3 11.5 %all-to-all-start = ((s32[32,1,1]{2,1,0:T(1,128)}), s32[32,1,1]{2,1,0:T(1,128)S(1)}, u32[]{:S(2)}, u32[]{:S(2)}) async-start(s32[32,1,1]{2,1,0:T(1,128)} %copy.29), calls=%async_computation | async-start | bytes 32768 | tf_op jit(solution)/shard_map/all_to_all | solution.py:72
  21.8 1.4 convolution_convert_fusion.4
  23.2 1.1 copy.30
  24.3 7.2 %all-to-all-done = s32[32,1,1]{2,1,0:T(1,128)S(1)} async-done(((s32[32,1,1]{2,1,0:T(1,128)}), s32[32,1,1]{2,1,0:T(1,128)S(1)}, u32[]{:S(2)}, u32[]{:S(2)}) %all-to-all-start) | async-done | bytes 160 | tf_op jit(solution)/shard_map/all_to_all | solution.py:72
  31.5 3.9 %all-to-all-start.1 = ((bf16[32,6,1280]{2,1,0:T(8,128)(2,1)}), bf16[32,6,1280]{2,1,0:T(8,128)(2,1)S(1)}, u32[]{:S(2)}, u32[]{:S(2)}) async-start(bf16[32,6,1280]{2,1,0:T(8,128)(2,1)} %copy.30), calls=%async_computation.1 | async-start | bytes 1310720 | tf_op jit(solution)/shard_map/all_to_all | solution.py:71
  36.1 18.5 %all-to-all-done.1 = bf16[32,6,1280]{2,1,0:T(8,128)(2,1)S(1)} async-done(((bf16[32,6,1280]{2,1,0:T(8,128)(2,1)}), bf16[32,6,1280]{2,1,0:T(8,128)(2,1)S(1)}, u32[]{:S(2)}, u32[]{:S(2)}) %all-to-all-start.1) | async-done | bytes 491552 | tf_op jit(solution)/shard_map/all_to_all | solution.py:71
  54.6 1.1 constant_dynamic-update-slice_fusion.7
  61.5 4.9 %all-to-all-start.2 = ((bf16[32,48,1280]{2,0,1:T(8,128)(2,1)}), bf16[32,48,1280]{2,0,1:T(8,128)(2,1)}, u32[]{:S(2)}, u32[]{:S(2)}) async-start(bf16[32,48,1280]{2,0,1:T(8,128)(2,1)} %constant_dynamic-update-slice_fusion), calls=%async_computation.2 | async-start | bytes 7864320 | tf_op jit(solution)/shard_map/all_to_all | solution.py:78
  66.4 2.7 %convert_reduce_fusion = f32[32,48]{1,0:T(8,128)S(1)} fusion(bf16[32,48,1280]{2,1,0:T(8,128)(2,1)} %param.10), kind=kLoop, calls=%fused_computation.17 | loop fusion | flops 3930624 | bytes 3938304 | tf_op jit(solution)/shard_map/reduce_sum | solution.py:85
  69.2 3.3 %multiply_reduce_fusion = f32[32,48]{1,0:T(8,128)S(1)} fusion(bf16[32,48,1280]{2,1,0:T(8,128)(2,1)} %param.10, f32[32,48]{1,0:T(8,128)S(1)} %broadcast_multiply_fusion), kind=kLoop, calls=%fused_computation.13 | loop fusion | flops 7862784 | bytes 3944448 | tf_op jit(solution)/shard_map/reduce_sum | solution.py:86
  72.6 2.9 %multiply_convert_fusion = bf16[1536,1280]{1,0:T(8,128)(2,1)S(1)} fusion(bf16[32,48,1280]{2,1,0:T(8,128)(2,1)} %param.10, f32[1280]{0:T(1024)S(1)} %copy-done.3, f32[1536]{0:T(1024)S(1)} %div.18, f32[1536]{0:T(1024)S(1)} %sqrt.6), kind=kLoop, calls=%fused_computation.12 | loop fusion | flops 9830400 | bytes 7881728 | tf_op jit(solution)/shard_map/convert_element_type | solution.py:89
  75.5 2.0 copy-done.2
  77.5 5.2 %fusion.34 = f32[1536,640]{1,0:T(8,128)} fusion(bf16[1536,1280]{1,0:T(8,128)(2,1)S(1)} %multiply_convert_fusion, bf16[1280,640]{1,0:T(8,128)(2,1)S(1)} %copy-done), kind=kOutput, calls=%fused_computation.64 | convolution fusion | flops 2516582400 | bytes 9502720 | tf_op jit(solution)/shard_map/dot_general | solution.py:90
  82.7 29.2 %all-to-all-done.2 = bf16[32,48,1280]{2,0,1:T(8,128)(2,1)} async-done(((bf16[32,48,1280]{2,0,1:T(8,128)(2,1)}), bf16[32,48,1280]{2,0,1:T(8,128)(2,1)}, u32[]{:S(2)}, u32[]{:S(2)}) %all-to-all-start.2) | async-done | bytes 3932192 | tf_op jit(solution)/shard_map/all_to_all | solution.py:78
  111.9 4.4 %copy.32 = bf16[32,48,1280]{2,1,0:T(8,128)(2,1)S(1)} copy(bf16[32,48,1280]{2,0,1:T(8,128)(2,1)} %all-to-all-done.2) | data formatting | bytes 7864320 | tf_op jit(solution)/shard_map/all_to_all | solution.py:78
  116.3 1.9 copy-done.1
  118.2 5.1 %convolution_convert_fusion.1 = bf16[640,1280]{0,1:T(8,128)(2,1)} fusion(bf16[1536,1280]{1,0:T(8,128)(2,1)S(1)} %bitcast.36, f32[1536,640]{1,0:T(8,128)S(1)} %copy-done.5), kind=kOutput, calls=%fused_computation.28 | convolution fusion | flops 2526248960 | bytes 9502720 | tf_op jit(solution)/shard_map/dot_general | solution.py:94
  123.6 8.2 %fusion.17 = bf16[1536,640]{1,0:T(8,128)(2,1)S(1)} fusion(f32[1536,640]{1,0:T(8,128)} %fusion.34, bf16[1536,1280]{1,0:T(8,128)(2,1)} %bitcast.37, bf16[640,1280]{1,0:T(8,128)(2,1)S(1)} %copy-done.4), kind=kOutput, calls=%fused_computation.26 | convolution fusion | flops 2535260160 | bytes 11468800 | tf_op jit(solution)/shard_map/dot_general | solution.py:92
  131.8 1.3 copy-done.6
  133.0 4.7 %convolution_convert_fusion = bf16[1536,1280]{1,0:T(8,128)(2,1)} fusion(bf16[1536,640]{1,0:T(8,128)(2,1)S(1)} %fusion.17, bf16[1280,640]{1,0:T(8,128)(2,1)S(1)} %copy-done), kind=kOutput, calls=%fused_computation.14 | convolution fusion | flops 2518548480 | bytes 7536640 | tf_op jit(solution)/shard_map/dot_general | solution.py:96
  137.8 7.2 %convolution_convert_fusion.2 = bf16[1280,640]{1,0:T(8,128)(2,1)} fusion(bf16[1536,1280]{1,0:T(8,128)(2,1)} %copy-done.2, bf16[1536,640]{1,0:T(8,128)(2,1)} %copy-done.6), kind=kOutput, calls=%fused_computation.29 | convolution fusion | flops 2517401600 | bytes 7536640 | tf_op jit(solution)/shard_map/dot_general | solution.py:95
  145.1 14.5 %reduce-scatter.11.cloned.1.call-done = bf16[640,160]{0,1:T(8,128)(2,1)} async-done(((bf16[640,1280]{0,1:T(8,128)(2,1)}), bf16[640,160]{0,1:T(8,128)(2,1)}) %reduce-scatter.11.cloned.1.call-update) | async-done | bytes 204816 | tf_op jit(solution)/shard_map/reduce_scatter | solution.py:16
  159.7 48.3 %all-reduce.4.cloned.1.call-done = bf16[1536,1280]{1,0:T(8,128)(2,1)} async-done(((bf16[1536,1280]{1,0:T(8,128)(2,1)}), bf16[1536,1280]{1,0:T(8,128)(2,1)}) %all-reduce.4.cloned.1.call-update) | async-done | bytes 3932176 | tf_op jit(solution)/shard_map/psum | solution.py:102
  208.0 5.8 %fusion.7 = (f32[1280]{0:T(1024)S(1)}, f32[1536]{0:T(1024)S(1)}, f32[1536]{0:T(1024)S(1)}) fusion(bf16[1536,1280]{1,0:T(8,128)(2,1)} %all-reduce.4.cloned.1.call-done, bf16[32,48,1280]{2,1,0:T(8,128)(2,1)} %param.10, f32[1536]{0:T(1024)S(1)} %div.18, f32[1536]{0:T(1024)S(1)} %sqrt.6, f32[1280]{0:T(1024)S(1)} %copy-done.3), kind=kLoop, calls=%fused_computation.9 | loop fusion | flops 19656448 | bytes 7899136 | tf_op jit(solution)/shard_map/reduce_sum | solution.py:103
  214.5 9.6 %all-to-all-start.3 = ((f32[32,1,1280]{2,1,0:T(1,128)}), f32[32,1,1280]{2,1,0:T(1,128)S(1)}, u32[]{:S(2)}, u32[]{:S(2)}) async-start(f32[32,1,1280]{2,1,0:T(1,128)} %broadcast_in_dim.38), calls=%async_computation.5 | async-start | bytes 327680 | tf_op jit(solution)/shard_map/all_to_all | solution.py:22
  224.7 6.1 %fusion.5 = bf16[1536,1280]{1,0:T(8,128)(2,1)S(1)} fusion(bf16[1536,1280]{1,0:T(8,128)(2,1)} %all-reduce.4.cloned.1.call-done, bf16[32,48,1280]{2,1,0:T(8,128)(2,1)} %param.10, f32[1536]{0:T(1024)S(1)} %get-tuple-element.9, f32[1536]{0:T(1024)S(1)} %get-tuple-element.10, f32[1280]{0:T(1024)S(1)} %copy-done.3, f32[1536]{0:T(1024)S(1)} %div.18, ...), kind=kLoop, calls=%fused_computation.7 | loop fusion | flops 23592960 | bytes 15758336 | tf_op jit(solution)/shard_map/add | solution.py:107
  231.0 0.9 copy.40
  231.9 3.1 %all-to-all-done.3 = f32[32,1,1280]{2,1,0:T(1,128)S(1)} async-done(((f32[32,1,1280]{2,1,0:T(1,128)}), f32[32,1,1280]{2,1,0:T(1,128)S(1)}, u32[]{:S(2)}, u32[]{:S(2)}) %all-to-all-start.3) | async-done | bytes 163872 | tf_op jit(solution)/shard_map/all_to_all | solution.py:22
  235.7 1.5 convert_element_type.66
  237.1 15.1 %reduce-scatter.13.cloned.1.call-done = bf16[40,640]{1,0:T(8,128)(2,1)} async-done(((bf16[160,640]{1,0:T(8,128)(2,1)}), bf16[40,640]{1,0:T(8,128)(2,1)}) %reduce-scatter.13.cloned.1.call-update) | async-done | bytes 51216
  252.2 1.5 convert_element_type.63
  (42 shorter events, 10.7 us)
Async XLA Ops:
  8.0 69.5 %copy-start = (bf16[1280,640]{1,0:T(8,128)(2,1)S(1)}, bf16[1280,640]{1,0:T(8,128)(2,1)}, u32[]{:S(2)}) copy-start(bf16[1280,640]{1,0:T(8,128)(2,1)} %param.11) | copy-start | bytes 4915204
  10.3 21.2 %all-to-all-start = ((s32[32,1,1]{2,1,0:T(1,128)}), s32[32,1,1]{2,1,0:T(1,128)S(1)}, u32[]{:S(2)}, u32[]{:S(2)}) async-start(s32[32,1,1]{2,1,0:T(1,128)} %copy.29), calls=%async_computation | async-start | bytes 32768 | tf_op jit(solution)/shard_map/all_to_all | solution.py:72
  31.5 23.1 %all-to-all-start.1 = ((bf16[32,6,1280]{2,1,0:T(8,128)(2,1)}), bf16[32,6,1280]{2,1,0:T(8,128)(2,1)S(1)}, u32[]{:S(2)}, u32[]{:S(2)}) async-start(bf16[32,6,1280]{2,1,0:T(8,128)(2,1)} %copy.30), calls=%async_computation.1 | async-start | bytes 1310720 | tf_op jit(solution)/shard_map/all_to_all | solution.py:71
  61.5 50.4 %all-to-all-start.2 = ((bf16[32,48,1280]{2,0,1:T(8,128)(2,1)}), bf16[32,48,1280]{2,0,1:T(8,128)(2,1)}, u32[]{:S(2)}, u32[]{:S(2)}) async-start(bf16[32,48,1280]{2,0,1:T(8,128)(2,1)} %constant_dynamic-update-slice_fusion), calls=%async_computation.2 | async-start | bytes 7864320 | tf_op jit(solution)/shard_map/all_to_all | solution.py:78
  66.4 6.2 %copy-start.3 = (f32[1280]{0:T(1024)S(1)}, f32[1280]{0:T(1024)}, u32[]{:S(2)}) copy-start(f32[1280]{0:T(1024)} %param.13) | copy-start | bytes 15364
  66.4 93.2 %reduce-scatter.11.cloned.1.call-start = ((), (), s32[]{:S(2)}) async-start(), calls=%async_computation.10 | async-start | bytes 1843200 | tf_op jit(solution)/shard_map/reduce_scatter | solution.py:16
  75.5 2.0 copy-start.2
  111.9 6.3 %copy-start.5 = (f32[1536,640]{1,0:T(8,128)S(1)}, f32[1536,640]{1,0:T(8,128)}, u32[]{:S(2)}) copy-start(f32[1536,640]{1,0:T(8,128)} %fusion.34) | copy-start | bytes 11796484
  116.3 1.9 copy-start.1
  118.2 5.4 %copy-start.4 = (bf16[640,1280]{1,0:T(8,128)(2,1)S(1)}, bf16[640,1280]{1,0:T(8,128)(2,1)}, u32[]{:S(2)}) copy-start(bf16[640,1280]{1,0:T(8,128)(2,1)} %param.12) | copy-start | bytes 4915204
  123.3 84.7 %all-reduce.4.cloned.1.call-start = ((), (), s32[]{:S(2)}) async-start(), calls=%async_computation.8 | async-start | bytes 7864320 | tf_op jit(solution)/shard_map/psum | solution.py:102
  131.8 1.3 copy-start.6
  137.8 86.4 %reduce-scatter.9.cloned.1.call-start = ((), (), s32[]{:S(2)}) async-start(), calls=%async_computation.9 | async-start | bytes 1843200 | tf_op jit(solution)/shard_map/reduce_scatter | solution.py:16
  145.1 90.6 %reduce-scatter.15.cloned.1.call-start = ((), (), s32[]{:S(2)}) async-start(), calls=%async_computation.12 | async-start | bytes 256000
  214.5 20.5 %all-to-all-start.3 = ((f32[32,1,1280]{2,1,0:T(1,128)}), f32[32,1,1280]{2,1,0:T(1,128)S(1)}, u32[]{:S(2)}, u32[]{:S(2)}) async-start(f32[32,1,1280]{2,1,0:T(1,128)} %broadcast_in_dim.38), calls=%async_computation.5 | async-start | bytes 327680 | tf_op jit(solution)/shard_map/all_to_all | solution.py:22
  224.1 28.1 %reduce-scatter.13.cloned.1.call-start = ((), (), s32[]{:S(2)}) async-start(), calls=%async_computation.11 | async-start | bytes 256000
Sparse Core Ops, SparseCore 0:
  123.4 36.1 reduce-scatter.10
  162.2 39.5 reduce-scatter.8
  204.4 21.6 reduce-scatter.14
  228.5 23.6 reduce-scatter.12
Sparse Core Ops, SparseCore 1:
  137.9 70.0 all-reduce.3
